TPU v7x, 32 devices: a whole 2x2x4 slice. The times are simulated.
32 devices in a mesh: clip: 2 (over x), frame: 8 (over z, y), band: 2 (over core).
Axes of the slice: x: 2, y: 2, z: 4, core: 2. Of those that a mesh axis runs over, the one named last changes fastest.
Arguments:
- pixels: bfloat16 [16, 16, 32, 256], P(('clip', 'frame'), 'band'), parts along dimension 0, may hold values from -40 to 40
- gru_state: bfloat16 [16, 16, 32, 128], P(('clip', 'frame'), 'band'), parts along dimension 0, may hold values from -1 to 1
- tokens: bfloat16 [16, 1024, 256], P(('clip', 'frame'), 'band'), parts along dimension 0, may hold values from -30 to 30
- visible: int32 [16, 1024], P(('clip', 'frame'), 'band'), parts along dimension 0, may hold values from 0 to 1, as said below
- query_frame: int32 [2048], P(('clip', 'band')), parts along dimension 0, may hold values from 0 to 7, as said below
- pixel_query: bfloat16 [256, 256], replicated, may hold values from -2 to 2
- pixel_key: bfloat16 [256, 256], replicated, may hold values from -2 to 2
- pixel_value: bfloat16 [256, 256], replicated, may hold values from -0.375 to 0.375
- pixel_out: bfloat16 [256, 128], replicated, may hold values from -1.5 to 1.5
- time_query: bfloat16 [256, 256], replicated, may hold values from -2 to 2
- time_key: bfloat16 [256, 256], replicated, may hold values from -2 to 2
- time_value: bfloat16 [256, 256], replicated, may hold values from -0.375 to 0.375
- time_out: bfloat16 [256, 256], replicated, may hold values from -0.75 to 0.75
- gru_gates: bfloat16 [3, 3, 256, 256], replicated, may hold values from -0.125 to 0.125
- gru_candidate: bfloat16 [3, 3, 256, 128], replicated, may hold values from -0.125 to 0.125
Outputs:
- refined_state: bfloat16 [16, 16, 32, 128], P(('clip', 'frame'), 'band'), parts along dimension 0
- track_out: bfloat16 [16, 1024, 256], P(('clip', 'frame'), 'band'), parts along dimension 0
There are 2 independent parts, one for each index of `clip`. A program takes and returns all parts, laid end to end along the dimension named above; an argument that names none is the same for every part. Nothing has to cross between parts.
Inputs may be any that keep to these rules, and one draw needn't show every extreme that they name: Each track is visible in the frame named by its query frame index. `query_frame`: every frame is the query frame of exactly 128 tracks.
All inputs are finite; a program needn't handle non-finite values.
Results may differ from a plain program's by a relative error of at most 0.0095.
The roundings to bfloat16 on the way count: a program that leaves them out, or rounds other values in their place, can miss the bound.
Values may be sent and summed in bfloat16 or wider, within the bound.
A program may use at most 64 MiB of HBM per device.

v0:
```python
import math

import jax
import jax.numpy as jnp
from jax import lax
from jax.experimental import pallas as pl
from jax.experimental.pallas import tpu as pltpu
from jax.sharding import PartitionSpec as P

HEADS = 8
HEAD_DIM = 32
GRU_WIDTH = 128
ITERS = 2
LOGIT_SCALE = HEAD_DIM ** (-0.5) * math.log2(math.e)
MASKED = -1e30
GROUP = 16
MESH = pl.DeviceIdType.MESH
F32 = jnp.float32
BF16 = jnp.bfloat16
N_IN = 14
UNROLL = 4
BEFORE = 4


def dot(a, b):
    return jnp.dot(a, b, preferred_element_type=F32)


def dot_nt(a, b):
    return lax.dot_general(a, b, (((1,), (1,)), ((), ())), preferred_element_type=F32)


def iota(shape, dim):
    return lax.broadcasted_iota(jnp.int32, shape, dim)


def softmax_rows(scores, bias):
    scores = scores * LOGIT_SCALE + bias
    top = jnp.max(scores, axis=-1, keepdims=True)
    powers = jnp.exp2(scores - top)
    total = jnp.sum(powers, axis=-1, keepdims=True)
    return (powers * (1.0 / total)).astype(BF16)


def column_taps(x, columns):
    length = x.shape[0]
    col = lax.rem(iota(x.shape, 0), columns)
    left = jnp.where(col == 0, 0.0, pltpu.roll(x, 1, 0))
    right = jnp.where(col == columns - 1, 0.0, pltpu.roll(x, length - 1, 0))
    return jnp.concatenate([left.astype(BF16), x.astype(BF16), right.astype(BF16)], axis=1)


def interior_conv(x, w_ref, low, columns):
    width = x.shape[1]
    taps = column_taps(x, columns)
    zero = jnp.zeros((columns, taps.shape[1]), BF16)
    above = jnp.concatenate([zero, taps[:-columns]], axis=0)
    below = jnp.concatenate([taps[columns:], zero], axis=0)
    patches = jnp.concatenate([above, taps, below], axis=1)
    weight = w_ref[:, :, low : low + width, :]
    return dot(patches, weight.reshape(9 * width, weight.shape[3]))


def kernel(frames, bands, *refs):
    inputs, refs = refs[:N_IN], refs[N_IN:]
    (out_state, returned), refs = refs[:2], refs[2:]
    held, refs = refs[:N_IN], refs[N_IN:]
    (
        partner_tok,
        partner_vis,
        tok_all,
        vis_all,
        queries,
        keys,
        values,
        att_out,
        stages,
        halos,
        attended,
        tops,
        totals,
        acc_g,
        acc_c,
        ctx_g,
        ctx_c,
        in_sem,
        own_sem,
        partner_send,
        partner_recv,
        tok_send,
        tok_recv,
        vis_send,
        vis_recv,
        back_send,
        back_recv,
        back_own,
        halo_send,
        halo_recv,
    ) = refs
    (pix_h, gst_h, tok_h, vis_h) = inputs[:4]
    (pix, gst, tok, vis, qfr, wpq, wpk, wpv, wpo, wtq, wtk, wtv, wg, wc) = held
    me = lax.axis_index("frame")
    band = lax.axis_index("band")
    other = lax.rem(band + 1, bands)
    tracks, channels = tok.shape[1], tok.shape[2]
    mine = tracks // frames
    chunks, part_rows = tok_all.shape[0], tok_all.shape[2]
    rows, columns = pix.shape[1], pix.shape[2]
    pixels = rows * columns

    loads = [pltpu.make_async_copy(inputs[i], held[i], in_sem.at[i]) for i in range(N_IN)]
    for i in (2, 6, 7, 0, 5, 3, 8, 4, 9, 10, 11, 1, 12, 13):
        loads[i].start()

    barrier = pltpu.get_barrier_semaphore()
    for k in range(1, frames):
        pl.semaphore_signal(
            barrier, inc=1, device_id={"frame": lax.rem(me + k, frames)}, device_id_type=MESH
        )
    pl.semaphore_signal(barrier, inc=1, device_id={"band": other}, device_id_type=MESH)

    for i in (2, 6, 7):
        loads[i].wait()
    lane_head = lax.div(iota((1, channels), 1), HEAD_DIM)
    attended[...] = jnp.zeros_like(attended)
    tops[...] = jnp.zeros_like(tops)
    totals[...] = jnp.zeros_like(totals)

    def attend_half(half, track_rows, seen, middle=None):
        keys[...] = dot(track_rows, wpk[...]).astype(BF16)
        values[...] = dot(track_rows, wpv[...]).astype(BF16)
        bias = jnp.where(seen > 0, 0.0, MASKED)

        def pixel_head(h, carry):
            chosen = jnp.where(lane_head == h, 1.0, 0.0)
            scores = dot_nt(queries[...] * chosen.astype(BF16), keys[...])
            scores = scores * LOGIT_SCALE + bias
            top = jnp.max(scores, axis=-1, keepdims=True)
            powers = jnp.exp2(scores - top)
            total = jnp.sum(powers, axis=-1, keepdims=True)
            tops[half] += top * chosen
            totals[half] += total * chosen
            attended[half] += dot(powers.astype(BF16), values[...]) * chosen
            return carry

        if middle is None:
            lax.fori_loop(0, HEADS, pixel_head, 0, unroll=UNROLL)
        else:
            lax.fori_loop(0, BEFORE, pixel_head, 0, unroll=UNROLL)
            middle()
            lax.fori_loop(BEFORE, HEADS, pixel_head, 0, unroll=UNROLL)

    for i in (0, 5, 3):
        loads[i].wait()
    queries[...] = dot(pix[0].reshape(pixels, channels), wpq[...]).astype(BF16)

    def to_partner(src, dst, send, recv):
        return pltpu.make_async_remote_copy(
            src_ref=src,
            dst_ref=dst,
            send_sem=send,
            recv_sem=recv,
            device_id={"band": other},
            device_id_type=MESH,
        )

    def to_frame(k, src, dst, send, recv):
        return pltpu.make_async_remote_copy(
            src_ref=src,
            dst_ref=dst,
            send_sem=send,
            recv_sem=recv,
            device_id={"frame": lax.rem(me + k, frames)},
            device_id_type=MESH,
        )

    partner_copies = [
        to_partner(tok_h.at[0], partner_tok, partner_send.at[0], partner_recv.at[0]),
        to_partner(vis_h, partner_vis, partner_send.at[1], partner_recv.at[1]),
    ]
    edge_row = (1 - band) * (rows - 1)
    edge = pl.multiple_of(edge_row * columns, columns)
    halo_copies = [
        to_partner(gst_h.at[0, edge_row], halos.at[0], halo_send.at[0], halo_recv.at[0])
    ]
    order = sorted(range(1, frames), key=lambda k: -min(k, frames - k))
    vis_copies = [
        to_frame(k, vis_h, vis_all.at[me], vis_send.at[k], vis_recv.at[k]) for k in order
    ]
    tok_copies = []
    for c in range(chunks):
        for k in order:
            target = lax.rem(me + k, frames)
            start = pl.multiple_of(target * mine + c * part_rows, part_rows)
            tok_copies.append(
                to_frame(
                    k,
                    tok_h.at[0, pl.ds(start, part_rows)],
                    tok_all.at[c, me],
                    tok_send.at[c, k],
                    tok_recv.at[c, k],
                )
            )
    own_copies = [
        pltpu.make_async_copy(
            tok_h.at[0, pl.ds(pl.multiple_of(me * mine + c * part_rows, part_rows), part_rows)],
            tok_all.at[c, me],
            own_sem.at[c],
        )
        for c in range(chunks)
    ]
    own_copies.append(pltpu.make_async_copy(vis_h, vis_all.at[me], own_sem.at[chunks]))


    def start_sends():
        pl.semaphore_wait(barrier, frames)
        for copy in partner_copies:
            copy.start()
        for copy in vis_copies + tok_copies:
            copy.start()
        for copy in own_copies:
            copy.start()
        halo_copies[0].start()

    attend_half(0, tok[0], vis[...], start_sends)
    for copy in partner_copies:
        copy.wait_recv()
    attend_half(1, partner_tok[...], partner_vis[...])
    highest = jnp.maximum(tops[0], tops[1])
    share_0 = jnp.exp2(tops[0] - highest)
    share_1 = jnp.exp2(tops[1] - highest)
    merged = (attended[0] * share_0 + attended[1] * share_1) / (
        totals[0] * share_0 + totals[1] * share_1
    )
    loads[8].wait()
    context = dot(merged.astype(BF16), wpo[...]).astype(BF16)

    def share_edge(stage, value):
        stages[stage - 1, :, :] = value
        copy = to_partner(
            stages.at[stage - 1, pl.ds(edge, columns)],
            halos.at[stage],
            halo_send.at[stage],
            halo_recv.at[stage],
        )
        copy.start()
        halo_copies.append(copy)

    share_edge(1, context)

    for i in (4, 9, 10, 11):
        loads[i].wait()
    for copy in own_copies:
        copy.wait()
    for copy in vis_copies:
        copy.wait_recv()
    block = frames * GROUP
    picked_shape = (tracks, frames * mine)
    slot = iota(picked_shape, 1)
    picked = me * mine + lax.div(slot, block) * GROUP + lax.rem(slot, GROUP)
    pick = jnp.where(iota(picked_shape, 0) == picked, 1.0, 0.0).astype(BF16)
    slot_frame = lax.rem(lax.div(iota((frames, frames * mine), 1), GROUP), frames)
    vis_rows = dot(vis_all[...].reshape(frames, tracks).astype(F32).astype(BF16), pick)
    vis_row = jnp.sum(
        jnp.where(slot_frame == iota(slot_frame.shape, 0), vis_rows, 0.0), axis=0, keepdims=True
    )
    query_rows = jnp.broadcast_to(qfr[...].astype(F32), (GROUP, tracks)).astype(BF16)
    query_row = dot(query_rows, pick)[0:1]
    same = lax.rem(iota((block, block), 0), GROUP) == lax.rem(iota((block, block), 1), GROUP)
    key_frame = lax.div(iota((block, block), 1), GROUP).astype(F32)
    together = max(1, min(HEADS, 1024 // block))
    back_copies = []
    own_back = []

    def attend_time(c):
        for copy in tok_copies[c * (frames - 1) : (c + 1) * (frames - 1)]:
            copy.wait_recv()
        flat = tok_all[c].reshape(frames * part_rows, channels)
        t_q, t_k, t_v = [
            dot(flat, weight[...]).astype(BF16).reshape(frames, part_rows, channels)
            for weight in (wtq, wtk, wtv)
        ]
        for g in range(part_rows // GROUP):
            part = slice(g * GROUP, (g + 1) * GROUP)
            first_col = (c * (part_rows // GROUP) + g) * block
            cols = slice(first_col, first_col + block)
            q_g = t_q[:, part, :].reshape(block, channels)
            k_g = t_k[:, part, :].reshape(block, channels)
            v_g = t_v[:, part, :].reshape(block, channels)
            is_anchor = jnp.logical_and(same, key_frame == query_row[:, cols])
            anchor = dot(jnp.where(is_anchor, 1.0, 0.0).astype(BF16), q_g)
            joint = (q_g.astype(F32) + anchor).astype(BF16)
            allowed = jnp.logical_and(same, vis_row[:, cols] > 0.5)
            bias = jnp.where(allowed, 0.0, MASKED)
            biases = jnp.concatenate([bias] * together, axis=0)
            result = jnp.zeros((block, channels), F32)
            for first in range(0, HEADS, together):
                masks = [jnp.where(lane_head == first + h, 1.0, 0.0) for h in range(together)]
                stacked = jnp.concatenate([joint * m.astype(BF16) for m in masks], axis=0)
                weights = softmax_rows(dot_nt(stacked, k_g), biases)
                mixed = dot(weights, v_g)
                for h in range(together):
                    result = result + mixed[h * block : (h + 1) * block] * masks[h]
            att_out[c, :, part, :] = result.astype(BF16).reshape(frames, GROUP, channels)
        there = pl.ds(c * part_rows, part_rows)
        for k in order:
            target = lax.rem(me + k, frames)
            copy = to_frame(
                k,
                att_out.at[c, target],
                returned.at[me, there],
                back_send.at[c, k],
                back_recv.at[c, k],
            )
            copy.start()
            back_copies.append(copy)
        copy = pltpu.make_async_copy(att_out.at[c, me], returned.at[me, there], back_own.at[c])
        copy.start()
        own_back.append(copy)

    for c in range(chunks):
        attend_time(c)

    def add_halo(acc, stage, w_ref, low):
        taps = column_taps(halos[stage].astype(F32), columns)
        weight = w_ref[pl.ds((1 - band) * 2, 1), :, low : low + GRU_WIDTH, :]
        weight = weight.reshape(3 * GRU_WIDTH, weight.shape[3])
        acc[pl.ds(edge, columns), :] += dot(taps, weight)

    for i in (1, 12, 13):
        loads[i].wait()
    context_f32 = context.astype(F32)
    ctx_g[...] = interior_conv(context_f32, wg, GRU_WIDTH, columns)
    ctx_c[...] = interior_conv(context_f32, wc, GRU_WIDTH, columns)
    halo_copies[1].wait_recv()
    add_halo(ctx_g, 1, wg, GRU_WIDTH)
    add_halo(ctx_c, 1, wc, GRU_WIDTH)
    state = gst[0].reshape(pixels, GRU_WIDTH).astype(F32)
    state_stage = 0
    for iteration in range(ITERS):
        acc_g[...] = ctx_g[...] + interior_conv(state, wg, 0, columns)
        halo_copies[state_stage].wait_recv()
        add_halo(acc_g, state_stage, wg, 0)
        reset = jax.nn.sigmoid(acc_g[:, GRU_WIDTH:])
        reset_state = (reset * state).astype(BF16)
        share_edge(2 + 2 * iteration, reset_state)
        update = jax.nn.sigmoid(acc_g[:, :GRU_WIDTH])
        acc_c[...] = ctx_c[...] + interior_conv(reset_state.astype(F32), wc, 0, columns)
        halo_copies[2 + 2 * iteration].wait_recv()
        add_halo(acc_c, 2 + 2 * iteration, wc, 0)
        candidate = jnp.tanh(acc_c[...])
        new_state = ((1.0 - update) * state + update * candidate).astype(BF16)
        if iteration < ITERS - 1:
            state_stage = 3 + 2 * iteration
            share_edge(state_stage, new_state)
            state = new_state.astype(F32)
    out_state[...] = new_state.reshape(1, rows, columns, GRU_WIDTH)

    for copy in own_back:
        copy.wait()
    for copy in back_copies:
        copy.wait_recv()
    for copy in partner_copies + vis_copies + tok_copies + back_copies + halo_copies:
        copy.wait_send()


def finish(state, tok, returned, wto, out_state, out_track):
    out_state[...] = state[...]
    update = dot(returned[...].reshape(tok.shape[1], tok.shape[2]), wto[...])
    out_track[0] = (tok[0].astype(F32) + update).astype(BF16)


def on_device(frames, bands, *args):
    args = list(args)
    args[4] = args[4].reshape(1, -1)
    time_out = args.pop(12)
    pixels, gru_state, tokens, visible = args[:4]
    tracks, channels = tokens.shape[1:]
    mine = tracks // frames
    chunks = 2 if mine % (2 * GROUP) == 0 else 1
    part_rows = mine // chunks
    rows, columns = pixels.shape[1:3]
    count = rows * columns
    halo_stages = 1 + 2 * ITERS
    dma = pltpu.SemaphoreType.DMA
    scratch = [pltpu.VMEM(a.shape, a.dtype) for a in args] + [
        pltpu.VMEM((tracks, channels), BF16),
        pltpu.VMEM((1, tracks), jnp.int32),
        pltpu.VMEM((chunks, frames, part_rows, channels), BF16),
        pltpu.VMEM((frames, 1, tracks), jnp.int32),
        pltpu.VMEM((count, channels), BF16),
        pltpu.VMEM((tracks, channels), BF16),
        pltpu.VMEM((tracks, channels), BF16),
        pltpu.VMEM((chunks, frames, part_rows, channels), BF16),
        pltpu.VMEM((halo_stages - 1, count, GRU_WIDTH), BF16),
        pltpu.VMEM((halo_stages, columns, GRU_WIDTH), BF16),
        pltpu.VMEM((2, count, channels), F32),
        pltpu.VMEM((2, count, channels), F32),
        pltpu.VMEM((2, count, channels), F32),
        pltpu.VMEM((count, 2 * GRU_WIDTH), F32),
        pltpu.VMEM((count, GRU_WIDTH), F32),
        pltpu.VMEM((count, 2 * GRU_WIDTH), F32),
        pltpu.VMEM((count, GRU_WIDTH), F32),
        dma((N_IN,)),
        dma((chunks + 1,)),
        dma((2,)),
        dma((2,)),
        dma((chunks, frames)),
        dma((chunks, frames)),
        dma((frames,)),
        dma((frames,)),
        dma((chunks, frames)),
        dma((chunks, frames)),
        dma((chunks,)),
        dma((halo_stages,)),
        dma((halo_stages,)),
    ]

    def body(*refs):
        kernel(frames, bands, *refs)

    state, returned = pl.pallas_call(
        body,
        out_shape=(
            jax.ShapeDtypeStruct(gru_state.shape, BF16),
            jax.ShapeDtypeStruct((frames, mine, channels), BF16),
        ),
        in_specs=[pl.BlockSpec(memory_space=pl.ANY)] * N_IN,
        out_specs=(
            pl.BlockSpec(memory_space=pltpu.VMEM),
            pl.BlockSpec(memory_space=pl.ANY),
        ),
        scratch_shapes=scratch,
        compiler_params=pltpu.CompilerParams(collective_id=0, has_side_effects=True),
        name="track_step",
    )(*args)
    return pl.pallas_call(
        finish,
        out_shape=(
            jax.ShapeDtypeStruct(gru_state.shape, BF16),
            jax.ShapeDtypeStruct(tokens.shape, BF16),
        ),
        in_specs=[pl.BlockSpec(memory_space=pltpu.VMEM)] * 4,
        out_specs=(pl.BlockSpec(memory_space=pltpu.VMEM),) * 2,
        name="track_finish",
    )(state, tokens, returned, time_out)


def solution(mesh):
    frames, bands = mesh.shape["frame"], mesh.shape["band"]
    placed = (
        P(("clip", "frame"), "band", None, None),
        P(("clip", "frame"), "band", None, None),
        P(("clip", "frame"), "band", None),
        P(("clip", "frame"), "band"),
        P(("clip", "band")),
    ) + (P(),) * 10
    return jax.shard_map(
        lambda *args: on_device(frames, bands, *args),
        mesh=mesh,
        in_specs=placed,
        out_specs=(P(("clip", "frame"), "band", None, None), P(("clip", "frame"), "band", None)),
        check_vma=False,
    )
```

profile of v0, /device:TPU:0, one launch (start us, length us, event | category | flops | bytes accessed | tf_op | source)
XLA Modules:
  0.0 26.3 jit_solution(1034445344104575898)
XLA Ops:
  0.6 23.6 %track_step.1 = (bf16[1,8,32,128]{3,2,1,0:T(8,128)(2,1)}, bf16[8,64,256]{2,1,0:T(8,128)(2,1)}) custom-call(bf16[1,8,32,256]{3,2,1,0:T(8,128)(2,1)} %refs_0_.1, bf16[1,8,32,128]{3,2,1,0:T(8,128)(2,1)} %refs_1_.1, bf16[1,512,256]{2,1,0:T(8,128)(2,1)} %tok.1, s32[1,512]{1,0:T(1,128)} %refs_3_.1, s32[1,512]{1,0:T(1,128)} %bitcast.1, bf16[256,256]{1,0:T(8,128)(2,1)} %refs_5_.1, ...), custom_call_target="tpu_custom_call" | custom-call | tf_op jit(solution)/shard_map/track_step/pallas_call | solution.py:422
  24.2 2.0 %track_finish.1 = (bf16[1,8,32,128]{3,2,1,0:T(8,128)(2,1)}, bf16[1,512,256]{2,1,0:T(8,128)(2,1)}) custom-call(bf16[1,8,32,128]{3,2,1,0:T(8,128)(2,1)} %get-tuple-element.4.state, bf16[1,512,256]{2,1,0:T(8,128)(2,1)} %tok.1, bf16[8,64,256]{2,1,0:T(8,128)(2,1)} %get-tuple-element.5.returned, bf16[256,256]{1,0:T(8,128)(2,1)} %wto.1), custom_call_target="tpu_custom_call" | custom-call | tf_op jit(solution)/shard_map/track_finish/pallas_call | solution.py:437
where the time goes:
time: 26.4 us; the launch traced here: 26.3 us
  Pallas kernels  25.6 us (97%)
  between operations  0.64 us (2%)
    pallas_call x1, Pallas kernels, on_device(): pl.pallas_call(body, out_shape=(jax.ShapeDtypeStruct(gru_state.shape, BF1...  23.6 us
    pallas_call x1, Pallas kernels, on_device(): pl.pallas_call(finish, out_shape=(jax.ShapeDtypeStruct(gru_state.shape, B...  2.03 us

commit v1 on v0

v1 whole, which is shorter than its diff:
```python
import math

import jax
import jax.numpy as jnp
from jax import lax
from jax.experimental import pallas as pl
from jax.experimental.pallas import tpu as pltpu
from jax.sharding import PartitionSpec as P

HEADS = 8
HEAD_DIM = 32
GRU_WIDTH = 128
ITERS = 2
LOGIT_SCALE = HEAD_DIM ** (-0.5) * math.log2(math.e)
MASKED = -1e30
TILE = 8
LANES = 128
MESH = pl.DeviceIdType.MESH
F32 = jnp.float32
BF16 = jnp.bfloat16
N_IN = 15
UNROLL = 4
CHUNKS = 2


def dot(a, b):
    return jnp.dot(a, b, preferred_element_type=F32)


def dot_nt(a, b):
    return lax.dot_general(a, b, (((1,), (1,)), ((), ())), preferred_element_type=F32)


def iota(shape, dim):
    return lax.broadcasted_iota(jnp.int32, shape, dim)


def column_taps(x, columns):
    length = x.shape[0]
    col = lax.rem(iota(x.shape, 0), columns)
    left = jnp.where(col == 0, 0.0, pltpu.roll(x, 1, 0))
    right = jnp.where(col == columns - 1, 0.0, pltpu.roll(x, length - 1, 0))
    return jnp.concatenate([left.astype(BF16), x.astype(BF16), right.astype(BF16)], axis=1)


def interior_conv(x, w_ref, low, columns):
    width = x.shape[1]
    taps = column_taps(x, columns)
    zero = jnp.zeros((columns, taps.shape[1]), BF16)
    above = jnp.concatenate([zero, taps[:-columns]], axis=0)
    below = jnp.concatenate([taps[columns:], zero], axis=0)
    patches = jnp.concatenate([above, taps, below], axis=1)
    weight = w_ref[:, :, low : low + width, :]
    return dot(patches, weight.reshape(9 * width, weight.shape[3]))


def kernel(frames, bands, *refs):
    inputs, refs = refs[:N_IN], refs[N_IN:]
    (out_state, out_track), refs = refs[:2], refs[2:]
    (
        squares,
        pix,
        gst,
        tok,
        ints,
        wpo,
        wg,
        wc,
        partner_tok,
        partner_vis,
        tok_all,
        vis_all,
        queries,
        keys,
        values,
        att_out,
        returned,
        seen_bias,
        stages,
        halos,
        attended,
        tops,
        totals,
        acc_g,
        acc_c,
        ctx_g,
        ctx_c,
        state_new,
        track_new,
        load_sem,
        partner_send,
        partner_recv,
        tok_send,
        tok_recv,
        vis_send,
        vis_recv,
        back_send,
        back_recv,
        halo_send,
        halo_recv,
        out_sem,
    ) = refs
    (pix_h, gst_h, tok_h, vis_h, qfr_h) = inputs[:5]
    (wpq_h, wpk_h, wpv_h, wpo_h, wtq_h, wtk_h, wtv_h, wto_h, wg_h, wc_h) = inputs[5:]
    wpk, wpv, wpq, wtq, wtk, wtv, wto = [squares.at[i] for i in range(7)]
    vis, qfr = ints.at[0:1], ints.at[1:2]
    me = lax.axis_index("frame")
    band = lax.axis_index("band")
    other = lax.rem(band + 1, bands)
    tracks, channels = tok.shape[1], tok.shape[2]
    mine = tracks // frames
    chunks, part_rows = tok_all.shape[0], tok_all.shape[2]
    rows, columns = pix.shape[1], pix.shape[2]
    pixels = rows * columns

    barrier = pltpu.get_barrier_semaphore()
    for k in range(1, frames):
        pl.semaphore_signal(
            barrier, inc=1, device_id={"frame": lax.rem(me + k, frames)}, device_id_type=MESH
        )
    pl.semaphore_signal(barrier, inc=1, device_id={"band": other}, device_id_type=MESH)

    groups = (
        ((tok_h, tok), (wpk_h, wpk), (wpv_h, wpv)),
        ((pix_h, pix), (wpq_h, wpq)),
        ((vis_h, vis), (qfr_h, qfr)),
        ((wpo_h, wpo),),
        ((wtq_h, wtq), (wtk_h, wtk), (wtv_h, wtv), (wto_h, wto)),
        ((gst_h, gst),),
        ((wg_h, wg),),
        ((wc_h, wc),),
    )
    whole = (squares.at[0:4], squares.at[0:2], ints, wpo, squares.at[0:4], gst, wg, wc)
    for n, group in enumerate(groups):
        for src, dst in group:
            pltpu.make_async_copy(src, dst, load_sem.at[n]).start()

    def loaded(n):
        pltpu.make_async_copy(whole[n], whole[n], load_sem.at[n]).wait()

    def to_partner(src, dst, send, recv):
        return pltpu.make_async_remote_copy(
            src_ref=src,
            dst_ref=dst,
            send_sem=send,
            recv_sem=recv,
            device_id={"band": other},
            device_id_type=MESH,
        )

    def to_frame(target, src, dst, send, recv):
        return pltpu.make_async_remote_copy(
            src_ref=src,
            dst_ref=dst,
            send_sem=send,
            recv_sem=recv,
            device_id={"frame": target},
            device_id_type=MESH,
        )

    edge_row = (1 - band) * (rows - 1)
    edge = pl.multiple_of(edge_row * columns, columns)
    ring = sorted(range(1, frames), key=lambda k: -min(k, frames - k))

    def start_sends():
        with jax.named_scope("w_barrier"):
            pl.semaphore_wait(barrier, frames)
        to_partner(tok_h.at[0], partner_tok, partner_send, partner_recv.at[0]).start()
        to_partner(vis_h, partner_vis, vis_send, partner_recv.at[1]).start()
        for c in range(chunks):
            for k in ring:
                target = lax.rem(me + k, frames)
                start = pl.multiple_of(target * mine + c * part_rows, part_rows)
                rows_there = tok_h.at[0, pl.ds(start, part_rows)]
                to_frame(target, rows_there, tok_all.at[c, me], tok_send, tok_recv.at[c]).start()
            if c == 0:
                for k in ring:
                    target = lax.rem(me + k, frames)
                    to_frame(target, vis_h, vis_all.at[me], vis_send, vis_recv).start()
        for c in range(chunks):
            start = pl.multiple_of(me * mine + c * part_rows, part_rows)
            pltpu.make_async_copy(
                tok_h.at[0, pl.ds(start, part_rows)], tok_all.at[c, me], tok_recv.at[c]
            ).start()
        pltpu.make_async_copy(vis_h, vis_all.at[me], vis_recv).start()
        to_partner(gst_h.at[0, edge_row], halos.at[0], halo_send, halo_recv.at[0]).start()

    slot = jnp.where(me == 0, 2, jnp.where(me <= frames // 4, 1, 0))

    def at_slot(n):
        pl.when(slot == n)(start_sends)

    at_slot(0)
    with jax.named_scope("w_loads"):
        loaded(0)
    lane_head = lax.div(iota((1, channels), 1), HEAD_DIM)
    attended[...] = jnp.zeros_like(attended)
    tops[...] = jnp.zeros_like(tops)
    totals[...] = jnp.zeros_like(totals)

    def attend_half(half, track_rows, seen):
        keys[...] = dot(track_rows, wpk[...]).astype(BF16)
        values[...] = dot(track_rows, wpv[...]).astype(BF16)
        bias = jnp.where(seen > 0, 0.0, MASKED)

        def pixel_head(h, carry):
            chosen = jnp.where(lane_head == h, 1.0, 0.0)
            scores = dot_nt(queries[...] * chosen.astype(BF16), keys[...])
            scores = scores * LOGIT_SCALE + bias
            top = jnp.max(scores, axis=-1, keepdims=True)
            powers = jnp.exp2(scores - top)
            total = jnp.sum(powers, axis=-1, keepdims=True)
            tops[half] += top * chosen
            totals[half] += total * chosen
            attended[half] += dot(powers.astype(BF16), values[...]) * chosen
            return carry

        if half == 0:
            lax.fori_loop(0, HEADS // 2, pixel_head, 0, unroll=UNROLL)
            at_slot(1)
            lax.fori_loop(HEADS // 2, HEADS, pixel_head, 0, unroll=UNROLL)
            at_slot(2)
        else:
            lax.fori_loop(0, HEADS, pixel_head, 0, unroll=UNROLL)

    loaded(1)
    loaded(2)
    queries[...] = dot(pix[0].reshape(pixels, channels), wpq[...]).astype(BF16)

    with jax.named_scope("s_half0"):
        attend_half(0, tok[0], vis[...])
    with jax.named_scope("w_partner"):
        to_partner(tok_h.at[0], partner_tok, partner_send, partner_recv.at[0]).wait_recv()
        to_partner(vis_h, partner_vis, vis_send, partner_recv.at[1]).wait_recv()
    with jax.named_scope("s_half1"):
        attend_half(1, partner_tok[...], partner_vis[...])
    highest = jnp.maximum(tops[0], tops[1])
    share_0 = jnp.exp2(tops[0] - highest)
    share_1 = jnp.exp2(tops[1] - highest)
    merged = (attended[0] * share_0 + attended[1] * share_1) / (
        totals[0] * share_0 + totals[1] * share_1
    )
    loaded(3)
    context = dot(merged.astype(BF16), wpo[...]).astype(BF16)

    def share_edge(stage, value):
        stages[stage - 1, :, :] = value
        to_partner(
            stages.at[stage - 1, pl.ds(edge, columns)],
            halos.at[stage],
            halo_send,
            halo_recv.at[stage],
        ).start()

    def edge_here(stage):
        pltpu.make_async_copy(halos.at[stage], halos.at[stage], halo_recv.at[stage]).wait()

    share_edge(1, context)

    loaded(4)
    with jax.named_scope("w_vis"):
        pltpu.make_async_copy(vis_all, vis_all, vis_recv).wait()

    blocks = mine // TILE
    key_rows = HEADS * TILE
    pair = LANES // key_rows
    first_mine = me * mine
    picked = iota((tracks, mine), 0) == first_mine + iota((tracks, mine), 1)
    picked = jnp.where(picked, 1.0, 0.0).astype(BF16)
    seen_rows = vis_all[...].reshape(frames, tracks).astype(F32).astype(BF16)
    seen_mine = dot(seen_rows, picked).astype(BF16)
    spread_shape = (mine, blocks * LANES)
    slot = iota(spread_shape, 1)
    spread = iota(spread_shape, 0) == lax.div(slot, LANES) * TILE + lax.rem(slot, TILE)
    spread = jnp.where(spread, 1.0, 0.0).astype(BF16)
    hidden = (dot(seen_mine, spread) - 1.0) * -MASKED
    lane_slot = lax.div(iota((1, LANES), 1), key_rows)
    for g in range(0, frames, pair):
        row = hidden[g : g + 1]
        for k in range(1, pair):
            chosen = lax.rem(lax.div(iota(row.shape, 1), key_rows), pair) == k
            row = jnp.where(chosen, hidden[g + k : g + k + 1], row)
        seen_bias[g // pair : g // pair + 1, :] = row
    picked_rows = iota((mine, tracks), 1) == first_mine + iota((mine, tracks), 0)
    picked_rows = jnp.where(picked_rows, 1.0, 0.0).astype(BF16)
    query_rows = jnp.broadcast_to(qfr[...].astype(F32), (LANES, tracks)).astype(BF16)
    query_col = dot_nt(picked_rows, query_rows)
    same_track = iota((TILE, LANES), 0) == lax.rem(iota((TILE, LANES), 1), TILE)
    heads_half = LANES // HEAD_DIM
    head_masks = []
    for first in range(0, heads_half, 2):
        wanted = first + lax.div(iota((2 * TILE, LANES), 0), TILE)
        head_masks.append(
            jnp.where(lax.div(iota((2 * TILE, LANES), 1), HEAD_DIM) == wanted, 1.0, 0.0).astype(BF16)
        )
    empty = jnp.zeros((2 * TILE, LANES), BF16)
    halves = channels // LANES
    group = 2 * pair

    def by_head(values_32):
        doubled = jnp.concatenate([values_32, values_32], axis=0).astype(BF16)
        out = []
        for half in range(halves):
            part = doubled[:, half * LANES : (half + 1) * LANES]
            for mask in head_masks:
                pieces = [empty] * halves
                pieces[half] = part * mask
                out.append(jnp.concatenate(pieces, axis=1))
        return out

    def attend_time(c):
        with jax.named_scope("w_tok%d" % c):
            pltpu.make_async_copy(tok_all.at[c], tok_all.at[c], tok_recv.at[c]).wait()
        flat = tok_all[c].reshape(frames * part_rows, channels)
        t_q = dot(flat, wtq[...]).astype(BF16).astype(F32)
        t_k = dot(flat, wtk[...])
        t_v = dot(flat, wtv[...])
        results = []
        for tile in range(part_rows // TILE):
            block = c * (part_rows // TILE) + tile

            def frame_rows(x, f):
                return x[f * part_rows + tile * TILE : f * part_rows + (tile + 1) * TILE]

            asked = query_col[block * TILE : (block + 1) * TILE]
            asked = jnp.concatenate([asked] * halves, axis=1)
            q_frames = [frame_rows(t_q, f) for f in range(frames)]
            anchor = q_frames[0]
            for f in range(1, frames):
                anchor = jnp.where(asked == f, q_frames[f], anchor)
            joint = jnp.concatenate([q + anchor for q in q_frames], axis=0).astype(BF16)
            scores = []
            for g in range(0, frames, group):
                tile_keys = sum([by_head(frame_rows(t_k, g + k)) for k in range(group)], [])
                product = dot_nt(joint, jnp.concatenate(tile_keys, axis=0))
                for i in range(group // pair):
                    n = g // pair + i
                    bias = seen_bias[n : n + 1, block * LANES : (block + 1) * LANES]
                    scores.append(product[:, i * LANES : (i + 1) * LANES] * LOGIT_SCALE + bias)
            top = scores[0]
            for s in scores[1:]:
                top = jnp.maximum(top, s)
            for k in range(1, pair):
                top = jnp.maximum(top, pltpu.roll(top, k * key_rows, 1))
            powers = [jnp.exp2(s - top) for s in scores]
            total = powers[0]
            for p in powers[1:]:
                total = total + p
            turned = total
            for k in range(1, pair):
                total = total + pltpu.roll(turned, k * key_rows, 1)
            keep = jnp.concatenate([same_track] * frames, axis=0)
            inverse = jnp.where(keep, 1.0 / total, 0.0)
            weights = [(p * inverse).astype(BF16) for p in powers]
            result = None
            for g in range(0, frames, group):
                tile_values = sum([by_head(frame_rows(t_v, g + k)) for k in range(group)], [])
                first = g // pair
                part = dot(
                    jnp.concatenate(weights[first : first + group // pair], axis=1),
                    jnp.concatenate(tile_values, axis=0),
                )
                result = part if result is None else result + part
            results.append(result)
        for f in range(frames):
            att_out[c, f] = jnp.concatenate(
                [r[f * TILE : (f + 1) * TILE] for r in results], axis=0
            ).astype(BF16)
        for k in range(frames - 1):
            target = k + lax.div(k + frames - me, frames)
            to_frame(
                target, att_out.at[c, target], returned.at[c, me], back_send, back_recv.at[c]
            ).start()
        pltpu.make_async_copy(att_out.at[c, me], returned.at[c, me], back_recv.at[c]).start()

    for c in range(chunks):
        with jax.named_scope("s_time%d" % c):
            attend_time(c)

    def add_halo(acc, stage, w_ref, low):
        taps = column_taps(halos[stage].astype(F32), columns)
        weight = w_ref[pl.ds((1 - band) * 2, 1), :, low : low + GRU_WIDTH, :]
        weight = weight.reshape(3 * GRU_WIDTH, weight.shape[3])
        acc[pl.ds(edge, columns), :] += dot(taps, weight)

    for n in (5, 6, 7):
        loaded(n)
    context_f32 = context.astype(F32)
    with jax.named_scope("s_gctx"):
        ctx_g[...] = interior_conv(context_f32, wg, GRU_WIDTH, columns)
        ctx_c[...] = interior_conv(context_f32, wc, GRU_WIDTH, columns)
        edge_here(1)
        add_halo(ctx_g, 1, wg, GRU_WIDTH)
        add_halo(ctx_c, 1, wc, GRU_WIDTH)
    state = gst[0].reshape(pixels, GRU_WIDTH).astype(F32)
    state_stage = 0
    for iteration in range(ITERS):
        acc_g[...] = ctx_g[...] + interior_conv(state, wg, 0, columns)
        with jax.named_scope("w_hs%d" % iteration):
            edge_here(state_stage)
        add_halo(acc_g, state_stage, wg, 0)
        reset = jax.nn.sigmoid(acc_g[:, GRU_WIDTH:])
        reset_state = (reset * state).astype(BF16)
        share_edge(2 + 2 * iteration, reset_state)
        update = jax.nn.sigmoid(acc_g[:, :GRU_WIDTH])
        acc_c[...] = ctx_c[...] + interior_conv(reset_state.astype(F32), wc, 0, columns)
        with jax.named_scope("w_hr%d" % iteration):
            edge_here(2 + 2 * iteration)
        add_halo(acc_c, 2 + 2 * iteration, wc, 0)
        candidate = jnp.tanh(acc_c[...])
        new_state = ((1.0 - update) * state + update * candidate).astype(BF16)
        if iteration < ITERS - 1:
            state_stage = 3 + 2 * iteration
            share_edge(state_stage, new_state)
            state = new_state.astype(F32)
    state_new[...] = new_state.reshape(1, rows, columns, GRU_WIDTH)
    out_copies = [pltpu.make_async_copy(state_new, out_state, out_sem.at[0])]
    out_copies[0].start()

    for c in range(chunks):
        with jax.named_scope("w_back%d" % c):
            pltpu.make_async_copy(returned.at[c], returned.at[c], back_recv.at[c]).wait()
        with jax.named_scope("s_final%d" % c):
            update = dot(returned[c].reshape(frames * part_rows, channels), wto[...])
            for owner in range(frames):
                there = slice(owner * mine + c * part_rows, owner * mine + (c + 1) * part_rows)
                change = update[owner * part_rows : (owner + 1) * part_rows]
                track_new[0, there] = (tok[0, there].astype(F32) + change).astype(BF16)
    out_copies.append(pltpu.make_async_copy(track_new, out_track, out_sem.at[1]))
    out_copies[1].start()
    with jax.named_scope("w_out"):
        for copy in out_copies:
            copy.wait()
    with jax.named_scope("w_send"):
        sent = tok_all.at[:, 0 : frames - 1]
        to_partner(tok_h.at[0], partner_tok, partner_send, partner_recv.at[0]).wait_send()
        pltpu.make_async_copy(vis_all, vis_all, vis_send).wait()
        pltpu.make_async_copy(sent, sent, tok_send).wait()
        pltpu.make_async_copy(sent, sent, back_send).wait()
        pltpu.make_async_copy(halos, halos, halo_send).wait()


def deliver(state, track, out_state, out_track, sems):
    copies = [
        pltpu.make_async_copy(track, out_track, sems.at[0]),
        pltpu.make_async_copy(state, out_state, sems.at[1]),
    ]
    for copy in copies:
        copy.start()
    for copy in copies:
        copy.wait()


def on_device(frames, bands, *args):
    args = list(args)
    args[4] = args[4].reshape(1, -1)
    pixels, gru_state, tokens, visible = args[:4]
    tracks, channels = tokens.shape[1:]
    mine = tracks // frames
    chunks = CHUNKS if mine % (2 * CHUNKS * TILE) == 0 else 1
    part_rows = mine // chunks
    rows, columns = pixels.shape[1:3]
    count = rows * columns
    halo_stages = 1 + 2 * ITERS
    pair = LANES // (HEADS * TILE)
    dma = pltpu.SemaphoreType.DMA
    scratch = [
        pltpu.VMEM((7, channels, channels), BF16),
        pltpu.VMEM(pixels.shape, BF16),
        pltpu.VMEM(gru_state.shape, BF16),
        pltpu.VMEM(tokens.shape, BF16),
        pltpu.VMEM((2, tracks), jnp.int32),
        pltpu.VMEM(args[8].shape, BF16),
        pltpu.VMEM(args[13].shape, BF16),
        pltpu.VMEM(args[14].shape, BF16),
        pltpu.VMEM((tracks, channels), BF16),
        pltpu.VMEM((1, tracks), jnp.int32),
        pltpu.VMEM((chunks, frames, part_rows, channels), BF16),
        pltpu.VMEM((frames, 1, tracks), jnp.int32),
        pltpu.VMEM((count, channels), BF16),
        pltpu.VMEM((tracks, channels), BF16),
        pltpu.VMEM((tracks, channels), BF16),
        pltpu.VMEM((chunks, frames, part_rows, channels), BF16),
        pltpu.VMEM((chunks, frames, part_rows, channels), BF16),
        pltpu.VMEM((frames // pair, mine // TILE * LANES), F32),
        pltpu.VMEM((halo_stages - 1, count, GRU_WIDTH), BF16),
        pltpu.VMEM((halo_stages, columns, GRU_WIDTH), BF16),
        pltpu.VMEM((2, count, channels), F32),
        pltpu.VMEM((2, count, channels), F32),
        pltpu.VMEM((2, count, channels), F32),
        pltpu.VMEM((count, 2 * GRU_WIDTH), F32),
        pltpu.VMEM((count, GRU_WIDTH), F32),
        pltpu.VMEM((count, 2 * GRU_WIDTH), F32),
        pltpu.VMEM((count, GRU_WIDTH), F32),
        pltpu.VMEM(gru_state.shape, BF16),
        pltpu.VMEM(tokens.shape, BF16),
        dma((8,)),
        dma,
        dma((2,)),
        dma,
        dma((chunks,)),
        dma,
        dma,
        dma,
        dma((chunks,)),
        dma,
        dma((halo_stages,)),
        dma((2,)),
    ]

    def body(*refs):
        kernel(frames, bands, *refs)

    state, track = pl.pallas_call(
        body,
        out_shape=(
            pltpu.VMEM(gru_state.shape, BF16),
            pltpu.VMEM(tokens.shape, BF16),
        ),
        in_specs=[pl.BlockSpec(memory_space=pl.ANY)] * N_IN,
        out_specs=(pl.BlockSpec(memory_space=pl.ANY),) * 2,
        scratch_shapes=scratch,
        compiler_params=pltpu.CompilerParams(collective_id=0, has_side_effects=True),
        name="track_step",
    )(*args)
    return pl.pallas_call(
        deliver,
        out_shape=(
            jax.ShapeDtypeStruct(gru_state.shape, BF16),
            jax.ShapeDtypeStruct(tokens.shape, BF16),
        ),
        in_specs=[pl.BlockSpec(memory_space=pltpu.VMEM)] * 2,
        out_specs=(pl.BlockSpec(memory_space=pl.ANY),) * 2,
        scratch_shapes=[dma((2,))],
        name="track_deliver",
    )(pltpu.with_memory_space_constraint(state, pltpu.VMEM), pltpu.with_memory_space_constraint(track, pltpu.VMEM))


def solution(mesh):
    frames, bands = mesh.shape["frame"], mesh.shape["band"]
    placed = (
        P(("clip", "frame"), "band", None, None),
        P(("clip", "frame"), "band", None, None),
        P(("clip", "frame"), "band", None),
        P(("clip", "frame"), "band"),
        P(("clip", "band")),
    ) + (P(),) * 10
    return jax.shard_map(
        lambda *args: on_device(frames, bands, *args),
        mesh=mesh,
        in_specs=placed,
        out_specs=(P(("clip", "frame"), "band", None, None), P(("clip", "frame"), "band", None)),
        check_vma=False,
    )
```

time: 26.4 us -> 23.3 us (0.88)
  Pallas kernels: 25.6 us -> 22.5 us
    pallas_call x2, Pallas kernels: 25.6 us -> 22.5 us  [the longest x1 21.8 us: on_device(): pl.pallas_call(body, out_shape=(pltpu.VMEM(gru_state.shape, BF16), pltpu....]
where the time goes in v1:
time: 23.3 us; the launch traced here: 23.1 us
  Pallas kernels  22.5 us (97%)
  between operations  0.64 us (3%)
    pallas_call x1, Pallas kernels, on_device(): pl.pallas_call(body, out_shape=(pltpu.VMEM(gru_state.shape, BF16), pltpu....  21.8 us
    pallas_call x1, Pallas kernels, on_device(): pl.pallas_call(deliver, out_shape=(jax.ShapeDtypeStruct(gru_state.shape,...  0.73 us

profile of v1, /device:TPU:0, one launch (start us, length us, event | category | flops | bytes accessed | tf_op | source)
XLA Modules:
  0.0 23.1 jit_solution(10977328387441525672)
XLA Ops:
  0.6 21.8 %track_step.1 = (bf16[1,8,32,128]{3,2,1,0:T(8,128)(2,1)S(1)}, bf16[1,512,256]{2,1,0:T(8,128)(2,1)S(1)}) custom-call(bf16[1,8,32,256]{3,2,1,0:T(8,128)(2,1)} %refs_0_.1, bf16[1,8,32,128]{3,2,1,0:T(8,128)(2,1)} %refs_1_.1, bf16[1,512,256]{2,1,0:T(8,128)(2,1)} %refs_2_.1, s32[1,512]{1,0:T(1,128)} %refs_3_.1, s32[1,512]{1,0:T(1,128)} %bitcast.1, ...), custom_call_target="tpu_custom_call" | custom-call | tf_op jit(solution)/shard_map/track_step/pallas_call | solution.py:514
  22.4 0.7 %track_deliver.1 = (bf16[1,8,32,128]{3,2,1,0:T(8,128)(2,1)}, bf16[1,512,256]{2,1,0:T(8,128)(2,1)}) custom-call(bf16[1,8,32,128]{3,2,1,0:T(8,128)(2,1)S(1)} %get-tuple-element.4.state, bf16[1,512,256]{2,1,0:T(8,128)(2,1)S(1)} %get-tuple-element.5.track), custom_call_target="tpu_custom_call" | custom-call | tf_op jit(solution)/shard_map/track_deliver/pallas_call | solution.py:526

commit v2 on v1

--- a/solution.py
+++ b/solution.py
@@ -167,16 +167,15 @@
             pl.semaphore_wait(barrier, frames)
         to_partner(tok_h.at[0], partner_tok, partner_send, partner_recv.at[0]).start()
         to_partner(vis_h, partner_vis, vis_send, partner_recv.at[1]).start()
+        for k in ring:
+            target = lax.rem(me + k, frames)
+            to_frame(target, vis_h, vis_all.at[me], vis_send, vis_recv).start()
         for c in range(chunks):
             for k in ring:
                 target = lax.rem(me + k, frames)
                 start = pl.multiple_of(target * mine + c * part_rows, part_rows)
                 rows_there = tok_h.at[0, pl.ds(start, part_rows)]
                 to_frame(target, rows_there, tok_all.at[c, me], tok_send, tok_recv.at[c]).start()
-            if c == 0:
-                for k in ring:
-                    target = lax.rem(me + k, frames)
-                    to_frame(target, vis_h, vis_all.at[me], vis_send, vis_recv).start()
         for c in range(chunks):
             start = pl.multiple_of(me * mine + c * part_rows, part_rows)
             pltpu.make_async_copy(
@@ -193,6 +192,44 @@
     at_slot(0)
     with jax.named_scope("w_loads"):
         loaded(0)
+    def share_edge(stage, value):
+        stages[stage - 1, :, :] = value
+        to_partner(
+            stages.at[stage - 1, pl.ds(edge, columns)],
+            halos.at[stage],
+            halo_send,
+            halo_recv.at[stage],
+        ).start()
+
+    def edge_here(stage):
+        pltpu.make_async_copy(halos.at[stage], halos.at[stage], halo_recv.at[stage]).wait()
+
+    def add_halo(acc, stage, w_ref, low):
+        taps = column_taps(halos[stage].astype(F32), columns)
+        weight = w_ref[pl.ds((1 - band) * 2, 1), :, low : low + GRU_WIDTH, :]
+        weight = weight.reshape(3 * GRU_WIDTH, weight.shape[3])
+        acc[pl.ds(edge, columns), :] += dot(taps, weight)
+
+    def gates_of_state(state, stage):
+        acc_g[...] = interior_conv(state, wg, 0, columns)
+        edge_here(stage)
+        add_halo(acc_g, stage, wg, 0)
+
+    def reset_of(state, stage):
+        acc_g[...] += ctx_g[...]
+        reset = jax.nn.sigmoid(acc_g[:, GRU_WIDTH:])
+        reset_state = (reset * state).astype(BF16)
+        share_edge(stage, reset_state)
+        acc_c[...] = ctx_c[...] + interior_conv(reset_state.astype(F32), wc, 0, columns)
+
+    def state_after(state, stage):
+        update = jax.nn.sigmoid(acc_g[:, :GRU_WIDTH])
+        with jax.named_scope("w_hr%d" % stage):
+            edge_here(stage)
+        add_halo(acc_c, stage, wc, 0)
+        candidate = jnp.tanh(acc_c[...])
+        return ((1.0 - update) * state + update * candidate).astype(BF16)
+
     lane_head = lax.div(iota((1, channels), 1), HEAD_DIM)
     attended[...] = jnp.zeros_like(attended)
     tops[...] = jnp.zeros_like(tops)
@@ -229,6 +266,11 @@
 
     with jax.named_scope("s_half0"):
         attend_half(0, tok[0], vis[...])
+    for n in (5, 6, 7):
+        loaded(n)
+    state = gst[0].reshape(pixels, GRU_WIDTH).astype(F32)
+    with jax.named_scope("s_g0"):
+        gates_of_state(state, 0)
     with jax.named_scope("w_partner"):
         to_partner(tok_h.at[0], partner_tok, partner_send, partner_recv.at[0]).wait_recv()
         to_partner(vis_h, partner_vis, vis_send, partner_recv.at[1]).wait_recv()
@@ -243,19 +285,8 @@
     loaded(3)
     context = dot(merged.astype(BF16), wpo[...]).astype(BF16)
 
-    def share_edge(stage, value):
-        stages[stage - 1, :, :] = value
-        to_partner(
-            stages.at[stage - 1, pl.ds(edge, columns)],
-            halos.at[stage],
-            halo_send,
-            halo_recv.at[stage],
-        ).start()
-
-    def edge_here(stage):
-        pltpu.make_async_copy(halos.at[stage], halos.at[stage], halo_recv.at[stage]).wait()
-
     share_edge(1, context)
+
 
     loaded(4)
     with jax.named_scope("w_vis"):
@@ -315,13 +346,14 @@
         t_q = dot(flat, wtq[...]).astype(BF16).astype(F32)
         t_k = dot(flat, wtk[...])
         t_v = dot(flat, wtv[...])
-        results = []
-        for tile in range(part_rows // TILE):
-            block = c * (part_rows // TILE) + tile
+        tiles = range(part_rows // TILE)
+        products = []
+        for tile in tiles:
 
             def frame_rows(x, f):
                 return x[f * part_rows + tile * TILE : f * part_rows + (tile + 1) * TILE]
 
+            block = c * len(tiles) + tile
             asked = query_col[block * TILE : (block + 1) * TILE]
             asked = jnp.concatenate([asked] * halves, axis=1)
             q_frames = [frame_rows(t_q, f) for f in range(frames)]
@@ -329,19 +361,25 @@
             for f in range(1, frames):
                 anchor = jnp.where(asked == f, q_frames[f], anchor)
             joint = jnp.concatenate([q + anchor for q in q_frames], axis=0).astype(BF16)
-            scores = []
             for g in range(0, frames, group):
                 tile_keys = sum([by_head(frame_rows(t_k, g + k)) for k in range(group)], [])
-                product = dot_nt(joint, jnp.concatenate(tile_keys, axis=0))
-                for i in range(group // pair):
-                    n = g // pair + i
-                    bias = seen_bias[n : n + 1, block * LANES : (block + 1) * LANES]
-                    scores.append(product[:, i * LANES : (i + 1) * LANES] * LOGIT_SCALE + bias)
+                products.append(dot_nt(joint, jnp.concatenate(tile_keys, axis=0)))
+        weights = []
+        groups_of = frames // group
+        for tile in tiles:
+            block = c * len(tiles) + tile
+            scores = []
+            for n in range(frames // pair):
+                product = products[tile * groups_of + n * pair // group]
+                first = n * pair % group // pair * LANES
+                bias = seen_bias[n : n + 1, block * LANES : (block + 1) * LANES]
+                scores.append(product[:, first : first + LANES] * LOGIT_SCALE + bias)
             top = scores[0]
             for s in scores[1:]:
                 top = jnp.maximum(top, s)
+            turned = top
             for k in range(1, pair):
-                top = jnp.maximum(top, pltpu.roll(top, k * key_rows, 1))
+                top = jnp.maximum(top, pltpu.roll(turned, k * key_rows, 1))
             powers = [jnp.exp2(s - top) for s in scores]
             total = powers[0]
             for p in powers[1:]:
@@ -351,17 +389,19 @@
                 total = total + pltpu.roll(turned, k * key_rows, 1)
             keep = jnp.concatenate([same_track] * frames, axis=0)
             inverse = jnp.where(keep, 1.0 / total, 0.0)
-            weights = [(p * inverse).astype(BF16) for p in powers]
-            result = None
-            for g in range(0, frames, group):
-                tile_values = sum([by_head(frame_rows(t_v, g + k)) for k in range(group)], [])
-                first = g // pair
-                part = dot(
-                    jnp.concatenate(weights[first : first + group // pair], axis=1),
-                    jnp.concatenate(tile_values, axis=0),
+            weights.append([(p * inverse).astype(BF16) for p in powers])
+        results = []
+        for tile in tiles:
+
+            def frame_rows(x, f):
+                return x[f * part_rows + tile * TILE : f * part_rows + (tile + 1) * TILE]
+
+            tile_values = sum([by_head(frame_rows(t_v, f)) for f in range(frames)], [])
+            results.append(
+                dot(
+                    jnp.concatenate(weights[tile], axis=1), jnp.concatenate(tile_values, axis=0)
                 )
-                result = part if result is None else result + part
-            results.append(result)
+            )
         for f in range(frames):
             att_out[c, f] = jnp.concatenate(
                 [r[f * TILE : (f + 1) * TILE] for r in results], axis=0
@@ -376,43 +416,29 @@
     for c in range(chunks):
         with jax.named_scope("s_time%d" % c):
             attend_time(c)
-
-    def add_halo(acc, stage, w_ref, low):
-        taps = column_taps(halos[stage].astype(F32), columns)
-        weight = w_ref[pl.ds((1 - band) * 2, 1), :, low : low + GRU_WIDTH, :]
-        weight = weight.reshape(3 * GRU_WIDTH, weight.shape[3])
-        acc[pl.ds(edge, columns), :] += dot(taps, weight)
-
-    for n in (5, 6, 7):
-        loaded(n)
     context_f32 = context.astype(F32)
     with jax.named_scope("s_gctx"):
         ctx_g[...] = interior_conv(context_f32, wg, GRU_WIDTH, columns)
         ctx_c[...] = interior_conv(context_f32, wc, GRU_WIDTH, columns)
+    with jax.named_scope("w_hctx"):
         edge_here(1)
-        add_halo(ctx_g, 1, wg, GRU_WIDTH)
-        add_halo(ctx_c, 1, wc, GRU_WIDTH)
-    state = gst[0].reshape(pixels, GRU_WIDTH).astype(F32)
-    state_stage = 0
-    for iteration in range(ITERS):
-        acc_g[...] = ctx_g[...] + interior_conv(state, wg, 0, columns)
-        with jax.named_scope("w_hs%d" % iteration):
-            edge_here(state_stage)
-        add_halo(acc_g, state_stage, wg, 0)
-        reset = jax.nn.sigmoid(acc_g[:, GRU_WIDTH:])
-        reset_state = (reset * state).astype(BF16)
-        share_edge(2 + 2 * iteration, reset_state)
-        update = jax.nn.sigmoid(acc_g[:, :GRU_WIDTH])
-        acc_c[...] = ctx_c[...] + interior_conv(reset_state.astype(F32), wc, 0, columns)
-        with jax.named_scope("w_hr%d" % iteration):
-            edge_here(2 + 2 * iteration)
-        add_halo(acc_c, 2 + 2 * iteration, wc, 0)
-        candidate = jnp.tanh(acc_c[...])
-        new_state = ((1.0 - update) * state + update * candidate).astype(BF16)
+    add_halo(ctx_g, 1, wg, GRU_WIDTH)
+    add_halo(ctx_c, 1, wc, GRU_WIDTH)
+    with jax.named_scope("s_reset1"):
+        reset_of(state, 2)
+    with jax.named_scope("s_state1"):
+        new_state = state_after(state, 2)
+    share_edge(3, new_state)
+
+    for iteration in range(1, ITERS):
+        state = new_state.astype(F32)
+        with jax.named_scope("s_g1"):
+            gates_of_state(state, 1 + 2 * iteration)
+            reset_of(state, 2 + 2 * iteration)
+        with jax.named_scope("s_state2"):
+            new_state = state_after(state, 2 + 2 * iteration)
         if iteration < ITERS - 1:
-            state_stage = 3 + 2 * iteration
-            share_edge(state_stage, new_state)
-            state = new_state.astype(F32)
+            share_edge(3 + 2 * iteration, new_state)
     state_new[...] = new_state.reshape(1, rows, columns, GRU_WIDTH)
     out_copies = [pltpu.make_async_copy(state_new, out_state, out_sem.at[0])]
     out_copies[0].start()

time: 23.3 us -> 21.6 us (0.927)
  Pallas kernels: 22.5 us -> 20.8 us
    pallas_call x1, Pallas kernels: 21.8 us -> 20.1 us  [on_device(): pl.pallas_call(body, out_shape=(pltpu.VMEM(gru_state.shape, BF16), pltpu....]
where the time goes in v2:
time: 21.6 us; the launch traced here: 21.4 us
  Pallas kernels  20.8 us (96%)
  between operations  0.64 us (3%)
    pallas_call x1, Pallas kernels, on_device(): pl.pallas_call(body, out_shape=(pltpu.VMEM(gru_state.shape, BF16), pltpu....  20.1 us
    pallas_call x1, Pallas kernels, on_device(): pl.pallas_call(deliver, out_shape=(jax.ShapeDtypeStruct(gru_state.shape,...  0.73 us

profile of v2, /device:TPU:0, one launch (start us, length us, event | category | flops | bytes accessed | tf_op | source)
XLA Modules:
  0.0 21.4 jit_solution(3290586290966306863)
XLA Ops:
  0.6 20.1 %track_step.1 = (bf16[1,8,32,128]{3,2,1,0:T(8,128)(2,1)S(1)}, bf16[1,512,256]{2,1,0:T(8,128)(2,1)S(1)}) custom-call(bf16[1,8,32,256]{3,2,1,0:T(8,128)(2,1)} %refs_0_.1, bf16[1,8,32,128]{3,2,1,0:T(8,128)(2,1)} %refs_1_.1, bf16[1,512,256]{2,1,0:T(8,128)(2,1)} %refs_2_.1, s32[1,512]{1,0:T(1,128)} %refs_3_.1, s32[1,512]{1,0:T(1,128)} %bitcast.1, ...), custom_call_target="tpu_custom_call" | custom-call | tf_op jit(solution)/shard_map/track_step/pallas_call | solution.py:540
  20.7 0.7 %track_deliver.1 = (bf16[1,8,32,128]{3,2,1,0:T(8,128)(2,1)}, bf16[1,512,256]{2,1,0:T(8,128)(2,1)}) custom-call(bf16[1,8,32,128]{3,2,1,0:T(8,128)(2,1)S(1)} %get-tuple-element.4.state, bf16[1,512,256]{2,1,0:T(8,128)(2,1)S(1)} %get-tuple-element.5.track), custom_call_target="tpu_custom_call" | custom-call | tf_op jit(solution)/shard_map/track_deliver/pallas_call | solution.py:552

commit v3 on v2

--- a/solution.py
+++ b/solution.py
@@ -25,6 +25,11 @@
 
 def dot(a, b):
     return jnp.dot(a, b, preferred_element_type=F32)
+
+
+def halves_dot(a, b):
+    half = a.shape[0] // 2
+    return jnp.concatenate([dot(a[:half], b), dot(a[half:], b)], axis=0)
 
 
 def dot_nt(a, b):
@@ -162,6 +167,17 @@
     edge = pl.multiple_of(edge_row * columns, columns)
     ring = sorted(range(1, frames), key=lambda k: -min(k, frames - k))
 
+    def send_tokens(parts):
+        for c in parts:
+            for k in ring:
+                target = lax.rem(me + k, frames)
+                start = pl.multiple_of(target * mine + c * part_rows, part_rows)
+                rows_there = tok_h.at[0, pl.ds(start, part_rows)]
+                to_frame(target, rows_there, tok_all.at[c, me], tok_send, tok_recv.at[c]).start()
+
+    def send_rest():
+        send_tokens(range(1, chunks))
+
     def start_sends():
         with jax.named_scope("w_barrier"):
             pl.semaphore_wait(barrier, frames)
@@ -170,12 +186,8 @@
         for k in ring:
             target = lax.rem(me + k, frames)
             to_frame(target, vis_h, vis_all.at[me], vis_send, vis_recv).start()
-        for c in range(chunks):
-            for k in ring:
-                target = lax.rem(me + k, frames)
-                start = pl.multiple_of(target * mine + c * part_rows, part_rows)
-                rows_there = tok_h.at[0, pl.ds(start, part_rows)]
-                to_frame(target, rows_there, tok_all.at[c, me], tok_send, tok_recv.at[c]).start()
+        send_tokens(range(1))
+        pl.when(band == 0)(send_rest)
         for c in range(chunks):
             start = pl.multiple_of(me * mine + c * part_rows, part_rows)
             pltpu.make_async_copy(
@@ -258,7 +270,9 @@
             lax.fori_loop(HEADS // 2, HEADS, pixel_head, 0, unroll=UNROLL)
             at_slot(2)
         else:
-            lax.fori_loop(0, HEADS, pixel_head, 0, unroll=UNROLL)
+            lax.fori_loop(0, HEADS // 2, pixel_head, 0, unroll=UNROLL)
+            pl.when(band > 0)(send_rest)
+            lax.fori_loop(HEADS // 2, HEADS, pixel_head, 0, unroll=UNROLL)
 
     loaded(1)
     loaded(2)
@@ -339,13 +353,21 @@
                 out.append(jnp.concatenate(pieces, axis=1))
         return out
 
+    late = range(frames // 4, frames // 2)
+    back_order = [[] for _ in range(chunks)]
+    for c in range(chunks - 1):
+        back_order[c] = [(c, n) for n in range(frames - 1) if n not in late]
+    back_order[-1] = [(chunks - 1, n) for n in range(frames // 4)]
+    back_order[-1] += [(c, n) for c in range(chunks - 1) for n in range(frames - 1) if n in late]
+    back_order[-1] += [(chunks - 1, n) for n in range(frames // 4, frames - 1)]
+
     def attend_time(c):
         with jax.named_scope("w_tok%d" % c):
             pltpu.make_async_copy(tok_all.at[c], tok_all.at[c], tok_recv.at[c]).wait()
         flat = tok_all[c].reshape(frames * part_rows, channels)
         t_q = dot(flat, wtq[...]).astype(BF16).astype(F32)
         t_k = dot(flat, wtk[...])
-        t_v = dot(flat, wtv[...])
+        t_v = halves_dot(flat, wtv[...])
         tiles = range(part_rows // TILE)
         products = []
         for tile in tiles:
@@ -406,12 +428,16 @@
             att_out[c, f] = jnp.concatenate(
                 [r[f * TILE : (f + 1) * TILE] for r in results], axis=0
             ).astype(BF16)
-        for k in range(frames - 1):
-            target = k + lax.div(k + frames - me, frames)
+        pltpu.make_async_copy(att_out.at[c, me], returned.at[c, me], back_recv.at[c]).start()
+        for part, n in back_order[c]:
+            target = n + lax.div(n + frames - me, frames)
             to_frame(
-                target, att_out.at[c, target], returned.at[c, me], back_send, back_recv.at[c]
+                target,
+                att_out.at[part, target],
+                returned.at[part, me],
+                back_send,
+                back_recv.at[part],
             ).start()
-        pltpu.make_async_copy(att_out.at[c, me], returned.at[c, me], back_recv.at[c]).start()
 
     for c in range(chunks):
         with jax.named_scope("s_time%d" % c):
@@ -447,7 +473,7 @@
         with jax.named_scope("w_back%d" % c):
             pltpu.make_async_copy(returned.at[c], returned.at[c], back_recv.at[c]).wait()
         with jax.named_scope("s_final%d" % c):
-            update = dot(returned[c].reshape(frames * part_rows, channels), wto[...])
+            update = halves_dot(returned[c].reshape(frames * part_rows, channels), wto[...])
             for owner in range(frames):
                 there = slice(owner * mine + c * part_rows, owner * mine + (c + 1) * part_rows)
                 change = update[owner * part_rows : (owner + 1) * part_rows]

time: 21.6 us -> 21.3 us (0.986)
  Pallas kernels: 20.8 us -> 20.5 us
    pallas_call x1, Pallas kernels: 20.1 us -> 19.7 us  [on_device(): pl.pallas_call(body, out_shape=(pltpu.VMEM(gru_state.shape, BF16), pltpu....]
where the time goes in v3:
time: 21.3 us; the launch traced here: 21.1 us
  Pallas kernels  20.5 us (96%)
  between operations  0.64 us (3%)
    pallas_call x1, Pallas kernels, on_device(): pl.pallas_call(body, out_shape=(pltpu.VMEM(gru_state.shape, BF16), pltpu....  19.7 us
    pallas_call x1, Pallas kernels, on_device(): pl.pallas_call(deliver, out_shape=(jax.ShapeDtypeStruct(gru_state.shape,...  0.73 us

profile of v3, /device:TPU:0, one launch (start us, length us, event | category | flops | bytes accessed | tf_op | source)
XLA Modules:
  0.0 21.1 jit_solution(16521818336154254010)
XLA Ops:
  0.6 19.7 %track_step.1 = (bf16[1,8,32,128]{3,2,1,0:T(8,128)(2,1)S(1)}, bf16[1,512,256]{2,1,0:T(8,128)(2,1)S(1)}) custom-call(bf16[1,8,32,256]{3,2,1,0:T(8,128)(2,1)} %refs_0_.1, bf16[1,8,32,128]{3,2,1,0:T(8,128)(2,1)} %refs_1_.1, bf16[1,512,256]{2,1,0:T(8,128)(2,1)} %refs_2_.1, s32[1,512]{1,0:T(1,128)} %refs_3_.1, s32[1,512]{1,0:T(1,128)} %bitcast.1, ...), custom_call_target="tpu_custom_call" | custom-call | tf_op jit(solution)/shard_map/track_step/pallas_call | solution.py:566
  20.4 0.7 %track_deliver.1 = (bf16[1,8,32,128]{3,2,1,0:T(8,128)(2,1)}, bf16[1,512,256]{2,1,0:T(8,128)(2,1)}) custom-call(bf16[1,8,32,128]{3,2,1,0:T(8,128)(2,1)S(1)} %get-tuple-element.4.state, bf16[1,512,256]{2,1,0:T(8,128)(2,1)S(1)} %get-tuple-element.5.track), custom_call_target="tpu_custom_call" | custom-call | tf_op jit(solution)/shard_map/track_deliver/pallas_call | solution.py:578

commit v4 on v3

--- a/solution.py
+++ b/solution.py
@@ -357,9 +357,22 @@
     back_order = [[] for _ in range(chunks)]
     for c in range(chunks - 1):
         back_order[c] = [(c, n) for n in range(frames - 1) if n not in late]
-    back_order[-1] = [(chunks - 1, n) for n in range(frames // 4)]
-    back_order[-1] += [(c, n) for c in range(chunks - 1) for n in range(frames - 1) if n in late]
-    back_order[-1] += [(chunks - 1, n) for n in range(frames // 4, frames - 1)]
+    back_order[-1] = [(chunks - 1, 0)]
+    back_order[-1] += [(chunks - 1, n) for n in range(frames // 2, frames - 1)]
+    back_later = [(chunks - 1, n) for n in range(1, frames // 4)]
+    back_later += [(c, n) for c in range(chunks - 1) for n in range(frames - 1) if n in late]
+    back_later += [(chunks - 1, n) for n in range(frames // 4, frames // 2)]
+
+    def send_back(pieces):
+        for part, n in pieces:
+            target = n + lax.div(n + frames - me, frames)
+            to_frame(
+                target,
+                att_out.at[part, target],
+                returned.at[part, me],
+                back_send,
+                back_recv.at[part],
+            ).start()
 
     def attend_time(c):
         with jax.named_scope("w_tok%d" % c):
@@ -429,15 +442,7 @@
                 [r[f * TILE : (f + 1) * TILE] for r in results], axis=0
             ).astype(BF16)
         pltpu.make_async_copy(att_out.at[c, me], returned.at[c, me], back_recv.at[c]).start()
-        for part, n in back_order[c]:
-            target = n + lax.div(n + frames - me, frames)
-            to_frame(
-                target,
-                att_out.at[part, target],
-                returned.at[part, me],
-                back_send,
-                back_recv.at[part],
-            ).start()
+        send_back(back_order[c])
 
     for c in range(chunks):
         with jax.named_scope("s_time%d" % c):
@@ -446,12 +451,14 @@
     with jax.named_scope("s_gctx"):
         ctx_g[...] = interior_conv(context_f32, wg, GRU_WIDTH, columns)
         ctx_c[...] = interior_conv(context_f32, wc, GRU_WIDTH, columns)
+    pl.when(band == 0)(lambda: send_back(back_later))
     with jax.named_scope("w_hctx"):
         edge_here(1)
     add_halo(ctx_g, 1, wg, GRU_WIDTH)
     add_halo(ctx_c, 1, wc, GRU_WIDTH)
     with jax.named_scope("s_reset1"):
         reset_of(state, 2)
+    pl.when(band > 0)(lambda: send_back(back_later))
     with jax.named_scope("s_state1"):
         new_state = state_after(state, 2)
     share_edge(3, new_state)

time: 21.3 us -> 21 us (0.986)
  Pallas kernels: 20.5 us -> 20.2 us
    pallas_call x1, Pallas kernels: 19.7 us -> 19.5 us  [on_device(): pl.pallas_call(body, out_shape=(pltpu.VMEM(gru_state.shape, BF16), pltpu....]
where the time goes in v4:
time: 21 us; the launch traced here: 20.8 us
  Pallas kernels  20.2 us (96%)
  between operations  0.64 us (3%)
    pallas_call x1, Pallas kernels, on_device(): pl.pallas_call(body, out_shape=(pltpu.VMEM(gru_state.shape, BF16), pltpu....  19.5 us
    pallas_call x1, Pallas kernels, on_device(): pl.pallas_call(deliver, out_shape=(jax.ShapeDtypeStruct(gru_state.shape,...  0.73 us

profile of v4, /device:TPU:0, one launch (start us, length us, event | category | flops | bytes accessed | tf_op | source)
XLA Modules:
  0.0 20.8 jit_solution(14835335856549495110)
XLA Ops:
  0.6 19.5 %track_step.1 = (bf16[1,8,32,128]{3,2,1,0:T(8,128)(2,1)S(1)}, bf16[1,512,256]{2,1,0:T(8,128)(2,1)S(1)}) custom-call(bf16[1,8,32,256]{3,2,1,0:T(8,128)(2,1)} %refs_0_.1, bf16[1,8,32,128]{3,2,1,0:T(8,128)(2,1)} %refs_1_.1, bf16[1,512,256]{2,1,0:T(8,128)(2,1)} %refs_2_.1, s32[1,512]{1,0:T(1,128)} %refs_3_.1, s32[1,512]{1,0:T(1,128)} %bitcast.1, ...), custom_call_target="tpu_custom_call" | custom-call | tf_op jit(solution)/shard_map/track_step/pallas_call | solution.py:573
  20.1 0.7 %track_deliver.1 = (bf16[1,8,32,128]{3,2,1,0:T(8,128)(2,1)}, bf16[1,512,256]{2,1,0:T(8,128)(2,1)}) custom-call(bf16[1,8,32,128]{3,2,1,0:T(8,128)(2,1)S(1)} %get-tuple-element.4.state, bf16[1,512,256]{2,1,0:T(8,128)(2,1)S(1)} %get-tuple-element.5.track), custom_call_target="tpu_custom_call" | custom-call | tf_op jit(solution)/shard_map/track_deliver/pallas_call | solution.py:585

commit v5 on v4

--- a/solution.py
+++ b/solution.py
@@ -500,14 +500,13 @@
 
 
 def deliver(state, track, out_state, out_track, sems):
-    copies = [
-        pltpu.make_async_copy(track, out_track, sems.at[0]),
-        pltpu.make_async_copy(state, out_state, sems.at[1]),
-    ]
-    for copy in copies:
-        copy.start()
-    for copy in copies:
-        copy.wait()
+    part = track.shape[1] // 4
+    for n in range(4):
+        there = pl.ds(n * part, part)
+        pltpu.make_async_copy(track.at[0, there], out_track.at[0, there], sems.at[0]).start()
+    pltpu.make_async_copy(state, out_state, sems.at[1]).start()
+    pltpu.make_async_copy(track, out_track, sems.at[0]).wait()
+    pltpu.make_async_copy(state, out_state, sems.at[1]).wait()
 
 
 def on_device(frames, bands, *args):

time: 21 us -> 21 us (level)
  no operation moved by 1% of the time
where the time goes in v5:
time: 21 us; the launch traced here: 20.8 us
  Pallas kernels  20.2 us (96%)
  between operations  0.64 us (3%)
    pallas_call x1, Pallas kernels, on_device(): pl.pallas_call(body, out_shape=(pltpu.VMEM(gru_state.shape, BF16), pltpu....  19.5 us
    pallas_call x1, Pallas kernels, on_device(): pl.pallas_call(deliver, out_shape=(jax.ShapeDtypeStruct(gru_state.shape,...  0.73 us

profile of v5, /device:TPU:0, one launch (start us, length us, event | category | flops | bytes accessed | tf_op | source)
XLA Modules:
  0.0 20.8 jit_solution(2899444904002208355)
XLA Ops:
  0.6 19.5 %track_step.1 = (bf16[1,8,32,128]{3,2,1,0:T(8,128)(2,1)S(1)}, bf16[1,512,256]{2,1,0:T(8,128)(2,1)S(1)}) custom-call(bf16[1,8,32,256]{3,2,1,0:T(8,128)(2,1)} %refs_0_.1, bf16[1,8,32,128]{3,2,1,0:T(8,128)(2,1)} %refs_1_.1, bf16[1,512,256]{2,1,0:T(8,128)(2,1)} %refs_2_.1, s32[1,512]{1,0:T(1,128)} %refs_3_.1, s32[1,512]{1,0:T(1,128)} %bitcast.1, ...), custom_call_target="tpu_custom_call" | custom-call | tf_op jit(solution)/shard_map/track_step/pallas_call | solution.py:572
  20.1 0.7 %track_deliver.1 = (bf16[1,8,32,128]{3,2,1,0:T(8,128)(2,1)}, bf16[1,512,256]{2,1,0:T(8,128)(2,1)}) custom-call(bf16[1,8,32,128]{3,2,1,0:T(8,128)(2,1)S(1)} %get-tuple-element.4.state, bf16[1,512,256]{2,1,0:T(8,128)(2,1)S(1)} %get-tuple-element.5.track), custom_call_target="tpu_custom_call" | custom-call | tf_op jit(solution)/shard_map/track_deliver/pallas_call | solution.py:584
